TPU v7x, 32 devices: a whole 2x2x4 slice. The times are simulated.
32 devices in a mesh: groups: 2 (over y), frame: 4 (over z), row: 2 (over core), head: 2 (over x).
Axes of the slice: x: 2, y: 2, z: 4, core: 2. Of those that a mesh axis runs over, the one named last changes fastest.
Arguments:
- queries: bfloat16 [8, 16, 48, 768], P(('groups', 'frame'), 'row', None, 'head'), parts along dimension 0, may hold values from -8 to 8
- keys: bfloat16 [8, 16, 48, 768], P(('groups', 'frame'), 'row', None, 'head'), parts along dimension 0, may hold values from -8 to 8
- values: bfloat16 [8, 16, 48, 768], P(('groups', 'frame'), 'row', None, 'head'), parts along dimension 0, may hold values from -6 to 6
- valid_prev: int32 [8, 16], P(('groups', 'frame'), 'row'), parts along dimension 0, may hold values 0 or 1
- mem_index: int32 [4], P('groups'), parts along dimension 0, may hold values from 0 to 3
Outputs:
- attended: bfloat16 [8, 16, 48, 768], P(('groups', 'frame'), 'row', None, 'head'), parts along dimension 0
There are 2 independent parts, one for each index of `groups`. A program takes and returns all parts, laid end to end along the dimension named above; each array names one. Nothing has to cross between parts.
All inputs are finite; a program needn't handle non-finite values. No bound on the sum of `valid_prev` on one device may be relied on, other than what follows from the above.
Results may differ from a plain program's by a relative error of at most 0.0085.
Values may be sent and summed in bfloat16 or wider, within the bound.
No kernel may reach another device: no remote copies, remote signals or barrier semaphores. Data moves between devices by JAX's collectives and lax.ppermute only.
A program may use at most 128 MiB of HBM per device.

v0:
```python
import functools

import jax
import jax.numpy as jnp
from jax import lax
from jax.experimental import pallas as pl
from jax.experimental.pallas import tpu as pltpu
from jax.sharding import PartitionSpec as P

HEAD_DIM = 128
WINDOW = 2
SCALE = HEAD_DIM**-0.5 * 1.4426950408889634
FLOOR = -1e30
BLOCK = 128
LOG2_3 = 1.584962500721156
LONG = 20_000_000_000
SHORT = 1000


def moved(block, pairs):
    return lax.ppermute(block, "frame", pairs)


def swapped(block):
    return lax.ppermute(block, "row", [(0, 1), (1, 0)])


def log2_weight(count):
    return jnp.where(
        count < 1, -jnp.inf, jnp.where(count < 2, 0.0, jnp.where(count < 3, 1.0, LOG2_3))
    ).astype(jnp.float32)


def attend_kernel(plan, windows, marked, n_f, fresh, finish, width, *refs):
    refs = list(refs)
    mem_ref, valid_ref, q_ref = refs[:3]
    frames = [refs[3 + 2 * f : 5 + 2 * f] for f in range(n_f)]
    acc, peaks = refs[-2:]
    queries, channels = frames[0][0].shape
    queries //= 2
    heads = channels // HEAD_DIM
    rows = queries // width
    band = lax.axis_index("row")
    z = lax.axis_index("frame")

    if fresh:
        acc[...] = jnp.zeros_like(acc)
        peaks[...] = jnp.full(peaks.shape, FLOOR, jnp.float32)
    ones = jnp.ones((2 * queries, HEAD_DIM), jnp.bfloat16)

    def step(f, times, window):
        factor = times.astype(jnp.float32)
        if window:
            outside, inside = log2_weight(times), log2_weight(times + 1)
            if marked:
                marks = q_ref[pl.ds(queries, 16), 0:HEAD_DIM].astype(jnp.float32)
            place = lax.broadcasted_iota(jnp.int32, (1, 2 * queries), 1)
            key_row = jnp.zeros((1, 2 * queries), jnp.int32)
            for r in range(1, 2 * rows):
                key_row = key_row + (place >= r * width).astype(jnp.int32)
            key_row = jnp.where(
                key_row < rows, key_row + band * rows, key_row - rows + (1 - band) * rows
            )
        for start in range(0, queries, BLOCK):
            part = pl.ds(start, BLOCK)
            if window:
                place = lax.broadcasted_iota(jnp.int32, (BLOCK, 1), 0) + start
                row = jnp.full((BLOCK, 1), -1000, jnp.int32)
                for r in range(rows):
                    here = (place >= r * width) & (place < (r + 1) * width)
                    if marked:
                        here = here & (marks[r : r + 1, 0:1] > 0.0)
                    else:
                        here = here & (valid_ref[0, r] > 0)
                    row = jnp.where(here, band * rows + r, row)
                bias = jnp.where(jnp.abs(key_row - row) <= WINDOW, inside, outside)
            for h in range(heads):
                lanes = pl.ds(h * HEAD_DIM, HEAD_DIM)
                key, value = [
                    jnp.concatenate([half[pl.ds(n * queries, queries), lanes] for half in frames[f]], 0)
                    for n in range(2)
                ]
                scores = (
                    lax.dot_general(
                        q_ref[part, lanes],
                        key,
                        (((1,), (1,)), ((), ())),
                        preferred_element_type=jnp.float32,
                    )
                    * SCALE
                )
                if window:
                    scores = scores + bias
                old = peaks[h, part, :]
                peak = jnp.maximum(old, jnp.max(scores, axis=1, keepdims=True))
                terms = jnp.exp2(scores - peak[:, 0:1]).astype(jnp.bfloat16)
                mixed = jnp.dot(
                    terms,
                    jnp.concatenate([value, ones], 1),
                    preferred_element_type=jnp.float32,
                )
                if not window:
                    mixed = mixed * factor
                fade = jnp.exp2(old - peak)
                acc[h, part, :] = acc[h, part, :] * jnp.concatenate([fade, fade], 1) + mixed
                peaks[h, part, :] = peak

    for f in range(n_f):
        times, window = plan(z, mem_ref[0], mem_ref[1], f)
        if windows[f]:
            pl.when(window)(functools.partial(step, f, times, True))
            pl.when((times > 0) & jnp.logical_not(window))(
                functools.partial(step, f, times, False)
            )
        else:
            pl.when(times > 0)(functools.partial(step, f, times, False))

    if finish:
        out = refs[-3]
        for h in range(heads):
            out[:, pl.ds(h * HEAD_DIM, HEAD_DIM)] = (
                acc[h, :, :HEAD_DIM] / acc[h, :, HEAD_DIM:]
            ).astype(jnp.bfloat16)


def attend(
    plan, windows, mem_index, valid, query, frames, state, finish, width, cost, marked=False
):
    tokens, channels = frames[0][0].shape
    tokens //= 2
    heads = channels // HEAD_DIM
    scalars = pl.BlockSpec(memory_space=pltpu.SMEM)
    whole = pl.BlockSpec(memory_space=pltpu.VMEM)
    operands = [mem_index, valid, query]
    for frame in frames:
        operands += frame
    shapes = [
        jax.ShapeDtypeStruct((heads, tokens, 2 * HEAD_DIM), jnp.float32),
        jax.ShapeDtypeStruct((heads, tokens, HEAD_DIM), jnp.float32),
    ]
    if finish:
        shapes = [jax.ShapeDtypeStruct((tokens, channels), jnp.bfloat16)] + shapes
    aliases, scratch = {}, []
    if finish and state is None:
        scratch = [pltpu.VMEM(s.shape, s.dtype) for s in shapes[1:]]
        shapes = shapes[:1]
    if state is not None:
        aliases = {len(operands) + n: len(shapes) - 2 + n for n in range(2)}
        operands += state
    outs = pl.pallas_call(
        functools.partial(
            attend_kernel,
            plan,
            windows,
            marked,
            len(frames),
            state is None,
            finish,
            width,
        ),
        in_specs=[scalars] * 2 + [whole] * (len(operands) - 2),
        out_specs=[whole] * len(shapes),
        out_shape=shapes,
        input_output_aliases=aliases,
        scratch_shapes=scratch,
        compiler_params=pltpu.CompilerParams(vmem_limit_bytes=16 << 20),
        cost_estimate=pl.CostEstimate(flops=cost, transcendentals=0, bytes_accessed=1000),
    )(*operands)
    return outs[0] if finish else list(outs)


def marker(mem_index):
    def kernel(mem_ref, out_ref):
        for n in range(mem_ref.shape[0]):
            out_ref[n] = mem_ref[n]

    scalars = pl.BlockSpec(memory_space=pltpu.SMEM)
    return pl.pallas_call(
        kernel,
        in_specs=[scalars],
        out_specs=scalars,
        out_shape=jax.ShapeDtypeStruct(mem_index.shape, jnp.int32),
        cost_estimate=pl.CostEstimate(flops=LONG, transcendentals=0, bytes_accessed=1000),
    )(mem_index)


def plan_four(query_set, names, z, first, second, f):
    middle = (z == 1) | (z == 2)
    ids = (z, 3 - z, 3 * (z - 1), 6 - 3 * z)
    mine, frame = ids[2 * query_set], ids[names[f]]
    times = (
        (frame == mine).astype(jnp.int32)
        + (first == frame).astype(jnp.int32)
        + (second == frame).astype(jnp.int32)
    )
    return jnp.where(middle, times, 0), middle & (frame == mine - 1)


def plan_any(z, first, second, f):
    return jnp.int32(0 if f == 1 else 1), z > 0


def four_frames(queries, keys, values, valid_prev, mem_index):
    shape = queries.shape
    width = shape[2]
    tokens = shape[1] * width

    def flat(block):
        return block.reshape(tokens, shape[3])

    query = flat(queries)
    inward = [(0, 1), (3, 2)]
    across = [(1, 2), (2, 1)]
    own = jnp.concatenate([flat(keys), flat(values)], 0)
    end = moved(own, inward)
    mid = moved(own, across)
    own = [own, swapped(own)]
    far = moved(end, across)
    marks = jnp.broadcast_to(valid_prev[0][:, None], (shape[1], shape[3])).astype(jnp.bfloat16)
    marks = jnp.pad(marks, ((0, 16 - shape[1]), (0, 0)))
    end_query = moved(jnp.concatenate([query, marks], 0), inward)
    mid = [mid, swapped(mid)]
    end = [end, swapped(end)]
    end_state = attend(
        functools.partial(plan_four, 1, (0, 1, 2)),
        (True, False, False),
        marker(mem_index),
        valid_prev,
        end_query,
        [own, mid, end],
        None,
        False,
        width,
        SHORT,
        marked=True,
    )
    far, end_state = lax.optimization_barrier((far, end_state))
    far = [far, swapped(far)]
    end_out = attend(
        functools.partial(plan_four, 1, (3,)),
        (False,),
        mem_index,
        valid_prev,
        end_query,
        [far],
        end_state,
        True,
        width,
        SHORT,
    )
    back = moved(end_out, [(1, 0), (2, 3)])
    out = attend(
        functools.partial(plan_four, 0, (0, 1, 2, 3)),
        (False, True, True, False),
        mem_index,
        valid_prev,
        query,
        [own, mid, end, far],
        None,
        True,
        width,
        LONG,
    )
    z = lax.axis_index("frame")
    return jnp.where((z == 1) | (z == 2), out, back).reshape(shape)


def any_frames(queries, keys, values, valid_prev, mem_index):
    shape = queries.shape
    width = shape[2]
    tokens = shape[1] * width
    count = lax.axis_size("frame")
    z = lax.axis_index("frame")

    def flat(block):
        return block.reshape(tokens, shape[3])

    own = jnp.concatenate([flat(keys), flat(values)], 0)
    before = moved(own, [(i, i + 1) for i in range(count - 1)])
    masked = jnp.stack([jnp.where(z == mem_index[s], own, jnp.zeros_like(own)) for s in range(2)])
    memory = lax.psum(masked, "frame")
    out = attend(
        plan_any,
        (False, True, False, False),
        mem_index,
        valid_prev,
        flat(queries),
        [[kv, swapped(kv)] for kv in (own, before, memory[0], memory[1])],
        None,
        True,
        width,
        LONG,
    )
    return out.reshape(shape)


def solution(mesh):
    spread = P(("groups", "frame"), "row", None, "head")
    body = four_frames if mesh.shape["frame"] == 4 else any_frames
    return jax.shard_map(
        body,
        mesh=mesh,
        in_specs=(spread, spread, spread, P(("groups", "frame"), "row"), P("groups")),
        out_specs=spread,
        check_vma=False,
    )
```

profile of v0, /device:TPU:0, one launch (start us, length us, event | category | flops | bytes accessed | tf_op | source)
XLA Modules:
  0.0 54.8 jit_solution(3137239829681895299)
XLA Ops:
  0.0 1.2 %pad_maximum_fusion.refs_3_ = bf16[768,384]{1,0:T(8,128)(2,1)S(1)} fusion(bf16[384,384]{1,0:T(8,128)(2,1)} %bitcast.8, bf16[384,384]{1,0:T(8,128)(2,1)} %bitcast.9), kind=kLoop, calls=%fused_computation | loop fusion | flops 1179648 | bytes 1179648 | tf_op jit(solution)/shard_map/concatenate | solution.py:214
  1.2 5.0 %collective-permute-start.3 = (bf16[768,384]{1,0:T(8,128)(2,1)S(1)}, bf16[768,384]{1,0:T(8,128)(2,1)S(1)}, u32[]{:S(2)}, u32[]{:S(2)}) collective-permute-start(bf16[768,384]{1,0:T(8,128)(2,1)S(1)} %pad_maximum_fusion.refs_3_), channel_id=1, source_target_pairs={{0,4},{12,8},{1,5},{13,9},{2,6},{14,10},{3,7},{15,11},{16,20},{28,... | collective-permute-start | bytes 1769480 | tf_op jit(solution)/shard_map/ppermute | solution.py:21
  6.1 0.7 %collective-permute-start.1 = (bf16[768,384]{1,0:T(8,128)(2,1)S(1)}, bf16[768,384]{1,0:T(8,128)(2,1)S(1)}, u32[]{:S(2)}, u32[]{:S(2)}) collective-permute-start(bf16[768,384]{1,0:T(8,128)(2,1)S(1)} %pad_maximum_fusion.refs_3_), channel_id=1, source_target_pairs={{4,8},{8,4},{5,9},{9,5},{6,10},{10,6},{7,11},{11,7},{20,24},{24,20... | collective-permute-start | bytes 1769480 | tf_op jit(solution)/shard_map/ppermute | solution.py:21
  6.8 0.1 collective-permute-start
  7.0 0.8 %pad_maximum_fusion.1 = bf16[400,384]{1,0:T(8,128)(2,1)} fusion(bf16[384,384]{1,0:T(8,128)(2,1)S(1)} %bitcast.6, bf16[400]{0:T(512)(128)(2,1)S(1)} %fusion), kind=kLoop, calls=%fused_computation.1 | loop fusion | flops 614400 | bytes 602912 | tf_op jit(solution)/shard_map/concatenate | solution.py:221
  7.8 4.0 %collective-permute-start.6 = (bf16[400,384]{1,0:T(8,128)(2,1)}, bf16[400,384]{1,0:T(8,128)(2,1)S(1)}, u32[]{:S(2)}, u32[]{:S(2)}) collective-permute-start(bf16[400,384]{1,0:T(8,128)(2,1)} %pad_maximum_fusion.1), channel_id=1, source_target_pairs={{0,4},{12,8},{1,5},{13,9},{2,6},{14,10},{3,7},{15,11},{16,20},{28,... | collective-permute-start | bytes 921608 | tf_op jit(solution)/shard_map/ppermute | solution.py:21
  11.9 8.0 %collective-permute-done.3.refs_7_ = bf16[768,384]{1,0:T(8,128)(2,1)S(1)} collective-permute-done((bf16[768,384]{1,0:T(8,128)(2,1)S(1)}, bf16[768,384]{1,0:T(8,128)(2,1)S(1)}, u32[]{:S(2)}, u32[]{:S(2)}) %collective-permute-start.3) | collective-permute-done | bytes 589856 | tf_op jit(solution)/shard_map/ppermute | solution.py:21
  19.8 0.0 collective-permute-start.4
  19.8 1.5 %collective-permute-start.5 = (bf16[768,384]{1,0:T(8,128)(2,1)S(1)}, bf16[768,384]{1,0:T(8,128)(2,1)}, u32[]{:S(2)}, u32[]{:S(2)}) collective-permute-start(bf16[768,384]{1,0:T(8,128)(2,1)S(1)} %collective-permute-done.3.refs_7_), channel_id=1, source_target_pairs={{4,8},{8,4},{5,9},{9,5},{6,10},{10,6},{7,11},{11,7},{20,24},{24,20... | collective-permute-start | bytes 1769480 | tf_op jit(solution)/shard_map/ppermute | solution.py:21
  21.3 0.0 collective-permute-done.1.refs_5_
  21.3 0.5 collective-permute-start.2
  21.8 1.2 %shard_map.55.refs_0_ = s32[2]{0:T(128)} custom-call(s32[2]{0:T(128)} %refs_0_.3), custom_call_target="tpu_custom_call" | custom-call | flops 20000000000 | bytes 1000 | tf_op jit(solution)/shard_map/pallas_call | solution.py:178
  23.0 2.3 %collective-permute-done.6.refs_2_ = bf16[400,384]{1,0:T(8,128)(2,1)S(1)} collective-permute-done((bf16[400,384]{1,0:T(8,128)(2,1)}, bf16[400,384]{1,0:T(8,128)(2,1)S(1)}, u32[]{:S(2)}, u32[]{:S(2)}) %collective-permute-start.6) | collective-permute-done | bytes 307232 | tf_op jit(solution)/shard_map/ppermute | solution.py:21
  25.4 0.0 collective-permute-done.refs_4_
  25.4 0.8 %copy-done = bf16[768,384]{1,0:T(8,128)(2,1)} copy-done((bf16[768,384]{1,0:T(8,128)(2,1)}, bf16[768,384]{1,0:T(8,128)(2,1)S(1)}, u32[]{:S(2)}) %copy-start) | copy-done | bytes 589848
  26.2 0.0 collective-permute-done.2.refs_6_
  26.2 0.0 collective-permute-done.4.refs_8_
  26.2 0.8 %copy-done.3 = bf16[768,384]{1,0:T(8,128)(2,1)} copy-done((bf16[768,384]{1,0:T(8,128)(2,1)}, bf16[768,384]{1,0:T(8,128)(2,1)S(1)}, u32[]{:S(2)}) %copy-start.3) | copy-done | bytes 589848
  27.0 1.1 %copy-done.1 = bf16[768,384]{1,0:T(8,128)(2,1)S(1)} copy-done((bf16[768,384]{1,0:T(8,128)(2,1)S(1)}, bf16[768,384]{1,0:T(8,128)(2,1)}, u32[]{:S(2)}) %copy-start.1) | copy-done | bytes 589848
  28.1 1.1 %copy-done.4 = bf16[768,384]{1,0:T(8,128)(2,1)S(1)} copy-done((bf16[768,384]{1,0:T(8,128)(2,1)S(1)}, bf16[768,384]{1,0:T(8,128)(2,1)}, u32[]{:S(2)}) %copy-start.4) | copy-done | bytes 589848
  29.1 0.7 %copy-done.11 = s32[2]{0:T(128)S(1)} copy-done((s32[2]{0:T(128)S(1)}, s32[2]{0:T(128)}, u32[]{:S(2)}) %copy-start.11) | copy-done | bytes 32
  29.8 1.2 %shard_map.56 = (f32[3,384,256]{2,1,0:T(8,128)S(1)}, f32[3,384,128]{2,1,0:T(8,128)S(1)}) custom-call(s32[2]{0:T(128)S(1)} %copy-done.11, s32[1,8]{1,0:T(1,128)S(1)} %copy-done.9, bf16[400,384]{1,0:T(8,128)(2,1)S(1)} %collective-permute-done.6.refs_2_, bf16[768,384]{1,0:T(8,128)(2,1)S(1)} %pad_maximum_fusion.refs_3_, bf16[768,384]{1,0:T(8,128)(2,1)S(1)} %copy-done.1, ...), custom_call_target="tpu_custom_call" | custom-call | flops 1000 | bytes 1000 | tf_op jit(solution)/shard_map/pallas_call | solution.py:150
  31.0 0.8 %copy-done.6 = f32[3,384,128]{2,1,0:T(8,128)} copy-done((f32[3,384,128]{2,1,0:T(8,128)}, f32[3,384,128]{2,1,0:T(8,128)S(1)}, u32[]{:S(2)}) %copy-start.6) | copy-done | bytes 589848
  31.8 0.0 collective-permute-done.5.refs_9_.refs_3_
  31.9 2.3 %collective-permute-done.7.refs_10_.refs_4_ = bf16[768,384]{1,0:T(8,128)(2,1)} collective-permute-done((bf16[768,384]{1,0:T(8,128)(2,1)}, bf16[768,384]{1,0:T(8,128)(2,1)}, u32[]{:S(2)}, u32[]{:S(2)}) %collective-permute-start.7) | collective-permute-done | bytes 589856 | tf_op jit(solution)/shard_map/ppermute | solution.py:25
  34.2 1.1 %copy-done.7 = f32[3,384,128]{2,1,0:T(8,128)S(1)} copy-done((f32[3,384,128]{2,1,0:T(8,128)S(1)}, f32[3,384,128]{2,1,0:T(8,128)}, u32[]{:S(2)}) %copy-start.7) | copy-done | bytes 589848
  35.3 0.7 %copy-done.10 = s32[2]{0:T(128)S(1)} copy-done((s32[2]{0:T(128)S(1)}, s32[2]{0:T(128)}, u32[]{:S(2)}) %copy-start.10) | copy-done | bytes 32
  35.9 1.4 %shard_map.58 = (bf16[384,384]{1,0:T(8,128)(2,1)S(1)}, f32[3,384,256]{2,1,0:T(8,128)S(1)}, f32[3,384,128]{2,1,0:T(8,128)S(1)}) custom-call(s32[2]{0:T(128)S(1)} %copy-done.10, s32[1,8]{1,0:T(1,128)S(1)} %copy-done.9, bf16[400,384]{1,0:T(8,128)(2,1)S(1)} %collective-permute-done.6.refs_2_, ...), custom_call_target="tpu_custom_call", output_to_operand_aliasing={{1}: (5, {}), {2}: (6, {})} | custom-call | flops 1000 | bytes 1000 | tf_op jit(solution)/shard_map/pallas_call | solution.py:150
  37.3 1.3 %collective-permute-start.8 = (bf16[384,384]{1,0:T(8,128)(2,1)S(1)}, bf16[384,384]{1,0:T(8,128)(2,1)S(1)}, u32[]{:S(2)}, u32[]{:S(2)}) collective-permute-start(bf16[384,384]{1,0:T(8,128)(2,1)S(1)} %get-tuple-element.16), channel_id=1, source_target_pairs={{4,0},{8,12},{5,1},{9,13},{6,2},{10,14},{7,3},{11,15},{20,16},{24,... | collective-permute-start | bytes 884744 | tf_op jit(solution)/shard_map/ppermute | solution.py:21
  38.6 1.9 %shard_map.57 = bf16[384,384]{1,0:T(8,128)(2,1)S(1)} custom-call(s32[2]{0:T(128)S(1)} %copy-done.10, s32[1,8]{1,0:T(1,128)S(1)} %copy-done.9, bf16[384,384]{1,0:T(8,128)(2,1)S(1)} %bitcast.7, bf16[768,384]{1,0:T(8,128)(2,1)S(1)} %pad_maximum_fusion.refs_3_, bf16[768,384]{1,0:T(8,128)(2,1)S(1)} %copy-done.2, ...), custom_call_target="tpu_custom_call" | custom-call | flops 20000000000 | bytes 1000 | tf_op jit(solution)/shard_map/pallas_call | solution.py:150
  40.5 13.6 %collective-permute-done.8 = bf16[384,384]{1,0:T(8,128)(2,1)S(1)} collective-permute-done((bf16[384,384]{1,0:T(8,128)(2,1)S(1)}, bf16[384,384]{1,0:T(8,128)(2,1)S(1)}, u32[]{:S(2)}, u32[]{:S(2)}) %collective-permute-start.8) | collective-permute-done | bytes 294944 | tf_op jit(solution)/shard_map/ppermute | solution.py:21
  54.0 0.8 %broadcast_select_fusion = bf16[384,384]{1,0:T(8,128)(2,1)} fusion(bf16[384,384]{1,0:T(8,128)(2,1)S(1)} %shard_map.57, bf16[384,384]{1,0:T(8,128)(2,1)S(1)} %collective-permute-done.8, pred[]{:T(512)S(6)} %or.3), kind=kLoop, calls=%fused_computation.2 | loop fusion | flops 147456 | bytes 884737 | tf_op jit(solution)/shard_map/jit(_where)/select_n | solution.py:265
  (19 shorter events, 0.0 us)
Async XLA Ops:
  0.0 6.9 %copy-start.9 = (s32[1,8]{1,0:T(1,128)S(1)}, s32[1,8]{1,0:T(1,128)}, u32[]{:S(2)}) copy-start(s32[1,8]{1,0:T(1,128)} %refs_1_.5) | copy-start | bytes 100
  0.0 7.0 %copy-start.8 = (bf16[1,8,48,384]{3,2,1,0:T(8,128)(2,1)S(1)}, bf16[1,8,48,384]{3,2,1,0:T(8,128)(2,1)}, u32[]{:S(2)}) copy-start(bf16[1,8,48,384]{3,2,1,0:T(8,128)(2,1)} %param.5) | copy-start | bytes 884740
  1.2 18.7 %collective-permute-start.3 = (bf16[768,384]{1,0:T(8,128)(2,1)S(1)}, bf16[768,384]{1,0:T(8,128)(2,1)S(1)}, u32[]{:S(2)}, u32[]{:S(2)}) collective-permute-start(bf16[768,384]{1,0:T(8,128)(2,1)S(1)} %pad_maximum_fusion.refs_3_), channel_id=1, source_target_pairs={{0,4},{12,8},{1,5},{13,9},{2,6},{14,10},{3,7},{15,11},{16,20},{28,... | collective-permute-start | bytes 1769480 | tf_op jit(solution)/shard_map/ppermute | solution.py:21
  6.1 15.2 %collective-permute-start.1 = (bf16[768,384]{1,0:T(8,128)(2,1)S(1)}, bf16[768,384]{1,0:T(8,128)(2,1)S(1)}, u32[]{:S(2)}, u32[]{:S(2)}) collective-permute-start(bf16[768,384]{1,0:T(8,128)(2,1)S(1)} %pad_maximum_fusion.refs_3_), channel_id=1, source_target_pairs={{4,8},{8,4},{5,9},{9,5},{6,10},{10,6},{7,11},{11,7},{20,24},{24,20... | collective-permute-start | bytes 1769480 | tf_op jit(solution)/shard_map/ppermute | solution.py:21
  6.8 18.5 %collective-permute-start = (bf16[768,384]{1,0:T(8,128)(2,1)S(1)}, bf16[768,384]{1,0:T(8,128)(2,1)S(1)}, u32[]{:S(2)}, u32[]{:S(2)}) collective-permute-start(bf16[768,384]{1,0:T(8,128)(2,1)S(1)} %pad_maximum_fusion.refs_3_), channel_id=1, source_target_pairs={{0,2},{2,0},{1,3},{3,1},{4,6},{6,4},{5,7},{7,5},{8,10},{10,8},{9,1... | collective-permute-start | bytes 1769480 | tf_op jit(solution)/shard_map/ppermute | solution.py:25
  7.8 17.6 %collective-permute-start.6 = (bf16[400,384]{1,0:T(8,128)(2,1)}, bf16[400,384]{1,0:T(8,128)(2,1)S(1)}, u32[]{:S(2)}, u32[]{:S(2)}) collective-permute-start(bf16[400,384]{1,0:T(8,128)(2,1)} %pad_maximum_fusion.1), channel_id=1, source_target_pairs={{0,4},{12,8},{1,5},{13,9},{2,6},{14,10},{3,7},{15,11},{16,20},{28,... | collective-permute-start | bytes 921608 | tf_op jit(solution)/shard_map/ppermute | solution.py:21
  19.8 6.4 %collective-permute-start.4 = (bf16[768,384]{1,0:T(8,128)(2,1)S(1)}, bf16[768,384]{1,0:T(8,128)(2,1)S(1)}, u32[]{:S(2)}, u32[]{:S(2)}) collective-permute-start(bf16[768,384]{1,0:T(8,128)(2,1)S(1)} %collective-permute-done.3.refs_7_), channel_id=1, source_target_pairs={{0,2},{2,0},{1,3},{3,1},{4,6},{6,4},{5,7},{7,5},{8,10},{10,8},{9,1... | collective-permute-start | bytes 1769480 | tf_op jit(solution)/shard_map/ppermute | solution.py:25
  19.8 12.0 %collective-permute-start.5 = (bf16[768,384]{1,0:T(8,128)(2,1)S(1)}, bf16[768,384]{1,0:T(8,128)(2,1)}, u32[]{:S(2)}, u32[]{:S(2)}) collective-permute-start(bf16[768,384]{1,0:T(8,128)(2,1)S(1)} %collective-permute-done.3.refs_7_), channel_id=1, source_target_pairs={{4,8},{8,4},{5,9},{9,5},{6,10},{10,6},{7,11},{11,7},{20,24},{24,20... | collective-permute-start | bytes 1769480 | tf_op jit(solution)/shard_map/ppermute | solution.py:21
  21.3 4.9 %collective-permute-start.2 = (bf16[768,384]{1,0:T(8,128)(2,1)S(1)}, bf16[768,384]{1,0:T(8,128)(2,1)}, u32[]{:S(2)}, u32[]{:S(2)}) collective-permute-start(bf16[768,384]{1,0:T(8,128)(2,1)S(1)} %collective-permute-done.1.refs_5_), channel_id=1, source_target_pairs={{0,2},{2,0},{1,3},{3,1},{4,6},{6,4},{5,7},{7,5},{8,10},{10,8},{9,1... | collective-permute-start | bytes 1769480 | tf_op jit(solution)/shard_map/ppermute | solution.py:25
  25.4 0.8 %copy-start = (bf16[768,384]{1,0:T(8,128)(2,1)}, bf16[768,384]{1,0:T(8,128)(2,1)S(1)}, u32[]{:S(2)}) copy-start(bf16[768,384]{1,0:T(8,128)(2,1)S(1)} %collective-permute-done.refs_4_) | copy-start | bytes 1769476
  26.2 0.8 %copy-start.3 = (bf16[768,384]{1,0:T(8,128)(2,1)}, bf16[768,384]{1,0:T(8,128)(2,1)S(1)}, u32[]{:S(2)}) copy-start(bf16[768,384]{1,0:T(8,128)(2,1)S(1)} %collective-permute-done.4.refs_8_) | copy-start | bytes 1769476
  27.0 1.1 %copy-start.1 = (bf16[768,384]{1,0:T(8,128)(2,1)S(1)}, bf16[768,384]{1,0:T(8,128)(2,1)}, u32[]{:S(2)}) copy-start(bf16[768,384]{1,0:T(8,128)(2,1)} %copy-done) | copy-start | bytes 1769476
  28.1 1.1 %copy-start.4 = (bf16[768,384]{1,0:T(8,128)(2,1)S(1)}, bf16[768,384]{1,0:T(8,128)(2,1)}, u32[]{:S(2)}) copy-start(bf16[768,384]{1,0:T(8,128)(2,1)} %copy-done.3) | copy-start | bytes 1769476
  29.1 0.7 %copy-start.11 = (s32[2]{0:T(128)S(1)}, s32[2]{0:T(128)}, u32[]{:S(2)}) copy-start(s32[2]{0:T(128)} %shard_map.55.refs_0_) | copy-start | bytes 28
  31.0 0.8 %copy-start.6 = (f32[3,384,128]{2,1,0:T(8,128)}, f32[3,384,128]{2,1,0:T(8,128)S(1)}, u32[]{:S(2)}) copy-start(f32[3,384,128]{2,1,0:T(8,128)S(1)} %get-tuple-element.15.refs_6_) | copy-start | bytes 1769476
  31.9 2.3 %collective-permute-start.7 = (bf16[768,384]{1,0:T(8,128)(2,1)}, bf16[768,384]{1,0:T(8,128)(2,1)}, u32[]{:S(2)}, u32[]{:S(2)}) collective-permute-start(bf16[768,384]{1,0:T(8,128)(2,1)} %collective-permute-done.5.refs_9_.refs_3_), channel_id=1, source_target_pairs={{0,2},{2,0},{1,3},{3,1},{4,6},{6,4},{5,7},{7,5},{8,10},{10,8},{9,1... | collective-permute-start | bytes 1769480 | tf_op jit(solution)/shard_map/ppermute | solution.py:25
  31.9 6.7 %copy-start.2 = (bf16[768,384]{1,0:T(8,128)(2,1)S(1)}, bf16[768,384]{1,0:T(8,128)(2,1)}, u32[]{:S(2)}) copy-start(bf16[768,384]{1,0:T(8,128)(2,1)} %copy-done) | copy-start | bytes 1769476
  31.9 6.7 %copy-start.5 = (bf16[768,384]{1,0:T(8,128)(2,1)S(1)}, bf16[768,384]{1,0:T(8,128)(2,1)}, u32[]{:S(2)}) copy-start(bf16[768,384]{1,0:T(8,128)(2,1)} %copy-done.3) | copy-start | bytes 1769476
  34.2 1.1 %copy-start.7 = (f32[3,384,128]{2,1,0:T(8,128)S(1)}, f32[3,384,128]{2,1,0:T(8,128)}, u32[]{:S(2)}) copy-start(f32[3,384,128]{2,1,0:T(8,128)} %copy-done.6) | copy-start | bytes 1769476
  35.3 0.7 %copy-start.10 = (s32[2]{0:T(128)S(1)}, s32[2]{0:T(128)}, u32[]{:S(2)}) copy-start(s32[2]{0:T(128)} %refs_0_.3) | copy-start | bytes 28
  37.3 16.8 %collective-permute-start.8 = (bf16[384,384]{1,0:T(8,128)(2,1)S(1)}, bf16[384,384]{1,0:T(8,128)(2,1)S(1)}, u32[]{:S(2)}, u32[]{:S(2)}) collective-permute-start(bf16[384,384]{1,0:T(8,128)(2,1)S(1)} %get-tuple-element.16), channel_id=1, source_target_pairs={{4,0},{8,12},{5,1},{9,13},{6,2},{10,14},{7,3},{11,15},{20,16},{24,... | collective-permute-start | bytes 884744 | tf_op jit(solution)/shard_map/ppermute | solution.py:21
where the time goes:
time: 55.7 us; the launch traced here: 54.8 us
  waiting for transfers between devices  26.2 us (47%)
  starting transfers between devices  13.1 us (24%)
  local copies, waits for them, and re-layouts  6.98 us (13%)
  Pallas kernels  5.61 us (10%)
  other arithmetic  2.76 us (5%)
    ppermute x5, waiting for transfers between devices, moved(): return lax.ppermute(block, 'frame', pairs)  23.9 us
    ppermute x5, starting transfers between devices, moved(): return lax.ppermute(block, 'frame', pairs)  12.5 us
    unnamed x24, local copies, waits for them, and re-layouts  6.98 us
    pallas_call x3, Pallas kernels, attend(): pl.pallas_call(functools.partial(attend_kernel, plan, windows, marked, le...  4.42 us
    ppermute x4, waiting for transfers between devices, swapped(): return lax.ppermute(block, 'row', [(0, 1), (1, 0)])  2.34 us
    pallas_call x1, Pallas kernels, marker(): pl.pallas_call(kernel, in_specs=[scalars], out_specs=scalars, out_shape=j...  1.18 us
    concatenate x1, other arithmetic, four_frames(): own = jnp.concatenate([flat(keys), flat(values)], 0)  1.16 us
  transfers between devices with their start and end apart: 9, of which 4 were waited for; matrix products, arithmetic and copies ran while one was open for 2% of the time, Pallas kernels for 8%

commit v1 on v0

--- a/solution.py
+++ b/solution.py
@@ -36,6 +36,7 @@
     mem_ref, valid_ref, q_ref = refs[:3]
     frames = [refs[3 + 2 * f : 5 + 2 * f] for f in range(n_f)]
     acc, peaks = refs[-2:]
+    lane = lax.broadcasted_iota(jnp.int32, (1, HEAD_DIM), 1)
     queries, channels = frames[0][0].shape
     queries //= 2
     heads = channels // HEAD_DIM
@@ -46,6 +47,13 @@
     if fresh:
         acc[...] = jnp.zeros_like(acc)
         peaks[...] = jnp.full(peaks.shape, FLOOR, jnp.float32)
+    else:
+        total, stat = refs[3 + 2 * n_f : 5 + 2 * n_f]
+        for h in range(heads):
+            acc[h, :, :HEAD_DIM] = total[:, pl.ds(h * HEAD_DIM, HEAD_DIM)]
+            shape = (queries, HEAD_DIM)
+            peaks[h] = jnp.broadcast_to(stat[:, h : h + 1], shape)
+            acc[h, :, HEAD_DIM:] = jnp.broadcast_to(stat[:, heads + h : heads + h + 1], shape)
     ones = jnp.ones((2 * queries, HEAD_DIM), jnp.bfloat16)
 
     def step(f, times, window):
@@ -121,6 +129,14 @@
             out[:, pl.ds(h * HEAD_DIM, HEAD_DIM)] = (
                 acc[h, :, :HEAD_DIM] / acc[h, :, HEAD_DIM:]
             ).astype(jnp.bfloat16)
+    else:
+        total, stat = refs[-4:-2]
+        packed = jnp.zeros((queries, HEAD_DIM), jnp.float32)
+        for h in range(heads):
+            total[:, pl.ds(h * HEAD_DIM, HEAD_DIM)] = acc[h, :, :HEAD_DIM]
+            packed = jnp.where(lane == h, peaks[h], packed)
+            packed = jnp.where(lane == heads + h, acc[h, :, HEAD_DIM:], packed)
+        stat[...] = packed
 
 
 def attend(
@@ -134,19 +150,14 @@
     operands = [mem_index, valid, query]
     for frame in frames:
         operands += frame
-    shapes = [
-        jax.ShapeDtypeStruct((heads, tokens, 2 * HEAD_DIM), jnp.float32),
-        jax.ShapeDtypeStruct((heads, tokens, HEAD_DIM), jnp.float32),
-    ]
-    if finish:
-        shapes = [jax.ShapeDtypeStruct((tokens, channels), jnp.bfloat16)] + shapes
-    aliases, scratch = {}, []
-    if finish and state is None:
-        scratch = [pltpu.VMEM(s.shape, s.dtype) for s in shapes[1:]]
-        shapes = shapes[:1]
     if state is not None:
-        aliases = {len(operands) + n: len(shapes) - 2 + n for n in range(2)}
         operands += state
+    shapes = [jax.ShapeDtypeStruct((tokens, channels), jnp.bfloat16)]
+    if not finish:
+        shapes = [
+            jax.ShapeDtypeStruct((tokens, channels), jnp.float32),
+            jax.ShapeDtypeStruct((tokens, HEAD_DIM), jnp.float32),
+        ]
     outs = pl.pallas_call(
         functools.partial(
             attend_kernel,
@@ -161,8 +172,10 @@
         in_specs=[scalars] * 2 + [whole] * (len(operands) - 2),
         out_specs=[whole] * len(shapes),
         out_shape=shapes,
-        input_output_aliases=aliases,
-        scratch_shapes=scratch,
+        scratch_shapes=[
+            pltpu.VMEM((heads, tokens, 2 * HEAD_DIM), jnp.float32),
+            pltpu.VMEM((heads, tokens, HEAD_DIM), jnp.float32),
+        ],
         compiler_params=pltpu.CompilerParams(vmem_limit_bytes=16 << 20),
         cost_estimate=pl.CostEstimate(flops=cost, transcendentals=0, bytes_accessed=1000),
     )(*operands)

time: 55.7 us -> 57.3 us (1.029); the launches traced: 54.8 us -> 57.8 us
  waiting for transfers between devices: 26.2 us -> 31 us
  local copies, waits for them, and re-layouts: 6.98 us -> 4.79 us
    ppermute x5, waiting for transfers between devices: 23.9 us -> 28.6 us  [moved(): return lax.ppermute(block, 'frame', pairs)]
    unnamed x24 -> x16, local copies, waits for them, and re-layouts: 6.98 us -> 4.79 us
  transfers between devices with their start and end apart: 9 -> 9, of which waited for: 4 -> 4; matrix products, arithmetic and copies ran while one was open for 2% -> 1% of each run, Pallas kernels for 8% -> 8%
where the time goes in v1:
time: 57.3 us; the launch traced here: 57.8 us
  waiting for transfers between devices  31 us (54%)
  starting transfers between devices  13.1 us (23%)
  Pallas kernels  6.06 us (11%)
  local copies, waits for them, and re-layouts  4.79 us (8%)
  other arithmetic  2.78 us (5%)
    ppermute x5, waiting for transfers between devices, moved(): return lax.ppermute(block, 'frame', pairs)  28.6 us
    ppermute x5, starting transfers between devices, moved(): return lax.ppermute(block, 'frame', pairs)  12.5 us
    pallas_call x3, Pallas kernels, attend(): pl.pallas_call(functools.partial(attend_kernel, plan, windows, marked, le...  4.88 us
    unnamed x16, local copies, waits for them, and re-layouts  4.79 us
    ppermute x4, waiting for transfers between devices, swapped(): return lax.ppermute(block, 'row', [(0, 1), (1, 0)])  2.35 us
    pallas_call x1, Pallas kernels, marker(): pl.pallas_call(kernel, in_specs=[scalars], out_specs=scalars, out_shape=j...  1.18 us
    concatenate x1, other arithmetic, four_frames(): own = jnp.concatenate([flat(keys), flat(values)], 0)  1.16 us
  transfers between devices with their start and end apart: 9, of which 4 were waited for; matrix products, arithmetic and copies ran while one was open for 1% of the time, Pallas kernels for 8%

profile of v1, /device:TPU:0, one launch (start us, length us, event | category | flops | bytes accessed | tf_op | source)
XLA Modules:
  0.0 57.8 jit_solution(4240452435181604995)
XLA Ops:
  0.0 1.2 %pad_maximum_fusion.refs_3_ = bf16[768,384]{1,0:T(8,128)(2,1)S(1)} fusion(bf16[384,384]{1,0:T(8,128)(2,1)} %bitcast.8, bf16[384,384]{1,0:T(8,128)(2,1)} %bitcast.9), kind=kLoop, calls=%fused_computation | loop fusion | flops 1179648 | bytes 1179648 | tf_op jit(solution)/shard_map/concatenate | solution.py:227
  1.2 5.0 %collective-permute-start.3 = (bf16[768,384]{1,0:T(8,128)(2,1)S(1)}, bf16[768,384]{1,0:T(8,128)(2,1)S(1)}, u32[]{:S(2)}, u32[]{:S(2)}) collective-permute-start(bf16[768,384]{1,0:T(8,128)(2,1)S(1)} %pad_maximum_fusion.refs_3_), channel_id=1, source_target_pairs={{0,4},{12,8},{1,5},{13,9},{2,6},{14,10},{3,7},{15,11},{16,20},{28,... | collective-permute-start | bytes 1769480 | tf_op jit(solution)/shard_map/ppermute | solution.py:21
  6.1 0.7 %collective-permute-start.1 = (bf16[768,384]{1,0:T(8,128)(2,1)S(1)}, bf16[768,384]{1,0:T(8,128)(2,1)S(1)}, u32[]{:S(2)}, u32[]{:S(2)}) collective-permute-start(bf16[768,384]{1,0:T(8,128)(2,1)S(1)} %pad_maximum_fusion.refs_3_), channel_id=1, source_target_pairs={{4,8},{8,4},{5,9},{9,5},{6,10},{10,6},{7,11},{11,7},{20,24},{24,20... | collective-permute-start | bytes 1769480 | tf_op jit(solution)/shard_map/ppermute | solution.py:21
  6.8 0.1 collective-permute-start
  7.0 0.8 %pad_maximum_fusion.1 = bf16[400,384]{1,0:T(8,128)(2,1)} fusion(bf16[384,384]{1,0:T(8,128)(2,1)S(1)} %bitcast.6, bf16[400]{0:T(512)(128)(2,1)S(1)} %fusion), kind=kLoop, calls=%fused_computation.1 | loop fusion | flops 614400 | bytes 602912 | tf_op jit(solution)/shard_map/concatenate | solution.py:234
  7.8 4.0 %collective-permute-start.6 = (bf16[400,384]{1,0:T(8,128)(2,1)}, bf16[400,384]{1,0:T(8,128)(2,1)S(1)}, u32[]{:S(2)}, u32[]{:S(2)}) collective-permute-start(bf16[400,384]{1,0:T(8,128)(2,1)} %pad_maximum_fusion.1), channel_id=1, source_target_pairs={{0,4},{12,8},{1,5},{13,9},{2,6},{14,10},{3,7},{15,11},{16,20},{28,... | collective-permute-start | bytes 921608 | tf_op jit(solution)/shard_map/ppermute | solution.py:21
  11.9 7.9 %collective-permute-done.3.refs_7_ = bf16[768,384]{1,0:T(8,128)(2,1)S(1)} collective-permute-done((bf16[768,384]{1,0:T(8,128)(2,1)S(1)}, bf16[768,384]{1,0:T(8,128)(2,1)S(1)}, u32[]{:S(2)}, u32[]{:S(2)}) %collective-permute-start.3) | collective-permute-done | bytes 589856 | tf_op jit(solution)/shard_map/ppermute | solution.py:21
  19.8 0.0 collective-permute-start.4
  19.8 1.5 %collective-permute-start.5 = (bf16[768,384]{1,0:T(8,128)(2,1)S(1)}, bf16[768,384]{1,0:T(8,128)(2,1)}, u32[]{:S(2)}, u32[]{:S(2)}) collective-permute-start(bf16[768,384]{1,0:T(8,128)(2,1)S(1)} %collective-permute-done.3.refs_7_), channel_id=1, source_target_pairs={{4,8},{8,4},{5,9},{9,5},{6,10},{10,6},{7,11},{11,7},{20,24},{24,20... | collective-permute-start | bytes 1769480 | tf_op jit(solution)/shard_map/ppermute | solution.py:21
  21.3 0.0 collective-permute-done.1.refs_5_
  21.3 0.5 collective-permute-start.2
  21.8 1.2 %shard_map.55.refs_0_ = s32[2]{0:T(128)} custom-call(s32[2]{0:T(128)} %refs_0_.3), custom_call_target="tpu_custom_call" | custom-call | flops 20000000000 | bytes 1000 | tf_op jit(solution)/shard_map/pallas_call | solution.py:191
  23.0 2.4 %collective-permute-done.6.refs_2_ = bf16[400,384]{1,0:T(8,128)(2,1)S(1)} collective-permute-done((bf16[400,384]{1,0:T(8,128)(2,1)}, bf16[400,384]{1,0:T(8,128)(2,1)S(1)}, u32[]{:S(2)}, u32[]{:S(2)}) %collective-permute-start.6) | collective-permute-done | bytes 307232 | tf_op jit(solution)/shard_map/ppermute | solution.py:21
  25.4 0.0 collective-permute-done.refs_4_
  25.4 0.0 collective-permute-done.4.refs_8_
  25.4 0.0 collective-permute-done.2.refs_6_
  25.4 0.0 copy-start.7
  25.4 0.6 %copy-done.7 = s32[2]{0:T(128)S(1)} copy-done((s32[2]{0:T(128)S(1)}, s32[2]{0:T(128)}, u32[]{:S(2)}) %copy-start.7) | copy-done | bytes 32
  26.0 1.3 %shard_map.56 = (f32[384,384]{1,0:T(8,128)S(1)}, f32[384,128]{1,0:T(8,128)S(1)}) custom-call(s32[2]{0:T(128)S(1)} %copy-done.7, s32[1,8]{1,0:T(1,128)S(1)} %copy-done.5, bf16[400,384]{1,0:T(8,128)(2,1)S(1)} %collective-permute-done.6.refs_2_, bf16[768,384]{1,0:T(8,128)(2,1)S(1)} %pad_maximum_fusion.refs_3_, ...), custom_call_target="tpu_custom_call" | custom-call | flops 1000 | bytes 1000 | tf_op jit(solution)/shard_map/pallas_call | solution.py:161
  27.4 0.8 %copy-done = f32[384,384]{1,0:T(8,128)} copy-done((f32[384,384]{1,0:T(8,128)}, f32[384,384]{1,0:T(8,128)S(1)}, u32[]{:S(2)}) %copy-start) | copy-done | bytes 589848
  28.2 0.7 %copy-done.3 = f32[384,128]{1,0:T(8,128)} copy-done((f32[384,128]{1,0:T(8,128)}, f32[384,128]{1,0:T(8,128)S(1)}, u32[]{:S(2)}) %copy-start.3) | copy-done | bytes 196632
  28.8 0.0 collective-permute-done.5.refs_9_.refs_3_
  28.8 0.0 collective-permute-start.7
  28.8 2.3 %collective-permute-done.7.refs_10_.refs_4_ = bf16[768,384]{1,0:T(8,128)(2,1)} collective-permute-done((bf16[768,384]{1,0:T(8,128)(2,1)}, bf16[768,384]{1,0:T(8,128)(2,1)}, u32[]{:S(2)}, u32[]{:S(2)}) %collective-permute-start.7) | collective-permute-done | bytes 589856 | tf_op jit(solution)/shard_map/ppermute | solution.py:25
  31.2 1.1 %copy-done.1 = f32[384,384]{1,0:T(8,128)S(1)} copy-done((f32[384,384]{1,0:T(8,128)S(1)}, f32[384,384]{1,0:T(8,128)}, u32[]{:S(2)}) %copy-start.1) | copy-done | bytes 589848
  32.3 0.9 %copy-done.4 = f32[384,128]{1,0:T(8,128)S(1)} copy-done((f32[384,128]{1,0:T(8,128)S(1)}, f32[384,128]{1,0:T(8,128)}, u32[]{:S(2)}) %copy-start.4) | copy-done | bytes 196632
  33.2 0.7 %copy-done.6 = s32[2]{0:T(128)S(1)} copy-done((s32[2]{0:T(128)S(1)}, s32[2]{0:T(128)}, u32[]{:S(2)}) %copy-start.6) | copy-done | bytes 32
  33.8 1.7 %shard_map.58 = bf16[384,384]{1,0:T(8,128)(2,1)S(1)} custom-call(s32[2]{0:T(128)S(1)} %copy-done.6, s32[1,8]{1,0:T(1,128)S(1)} %copy-done.5, bf16[400,384]{1,0:T(8,128)(2,1)S(1)} %collective-permute-done.6.refs_2_, bf16[768,384]{1,0:T(8,128)(2,1)} %collective-permute-done.5.refs_9_.refs_3_, bf16[768,384]{1,0:T(8,128)(2,1)} %collective-permute-done.7.refs_10_.refs_4_, ...), custom_call_target="tpu_custom_call" | custom-call | flops 1000 | bytes 1000 | tf_op jit(solution)/shard_map/pallas_call | solution.py:161
  35.6 1.3 %collective-permute-start.8 = (bf16[384,384]{1,0:T(8,128)(2,1)S(1)}, bf16[384,384]{1,0:T(8,128)(2,1)S(1)}, u32[]{:S(2)}, u32[]{:S(2)}) collective-permute-start(bf16[384,384]{1,0:T(8,128)(2,1)S(1)} %shard_map.58), channel_id=1, source_target_pairs={{4,0},{8,12},{5,1},{9,13},{6,2},{10,14},{7,3},{11,15},{20,16},{24,... | collective-permute-start | bytes 884744 | tf_op jit(solution)/shard_map/ppermute | solution.py:21
  36.9 1.9 %shard_map.57 = bf16[384,384]{1,0:T(8,128)(2,1)S(1)} custom-call(s32[2]{0:T(128)S(1)} %copy-done.6, s32[1,8]{1,0:T(1,128)S(1)} %copy-done.5, bf16[384,384]{1,0:T(8,128)(2,1)S(1)} %bitcast.7, bf16[768,384]{1,0:T(8,128)(2,1)S(1)} %pad_maximum_fusion.refs_3_, bf16[768,384]{1,0:T(8,128)(2,1)S(1)} %collective-permute-done.refs_4_, ...), custom_call_target="tpu_custom_call" | custom-call | flops 20000000000 | bytes 1000 | tf_op jit(solution)/shard_map/pallas_call | solution.py:161
  38.7 18.3 %collective-permute-done.8 = bf16[384,384]{1,0:T(8,128)(2,1)S(1)} collective-permute-done((bf16[384,384]{1,0:T(8,128)(2,1)S(1)}, bf16[384,384]{1,0:T(8,128)(2,1)S(1)}, u32[]{:S(2)}, u32[]{:S(2)}) %collective-permute-start.8) | collective-permute-done | bytes 294944 | tf_op jit(solution)/shard_map/ppermute | solution.py:21
  57.0 0.8 %broadcast_select_fusion = bf16[384,384]{1,0:T(8,128)(2,1)} fusion(bf16[384,384]{1,0:T(8,128)(2,1)S(1)} %shard_map.57, bf16[384,384]{1,0:T(8,128)(2,1)S(1)} %collective-permute-done.8, pred[]{:T(512)S(6)} %or.3), kind=kLoop, calls=%fused_computation.2 | loop fusion | flops 147456 | bytes 884737 | tf_op jit(solution)/shard_map/jit(_where)/select_n | solution.py:278
  (11 shorter events, 0.0 us)
Async XLA Ops:
  0.0 6.9 %copy-start.5 = (s32[1,8]{1,0:T(1,128)S(1)}, s32[1,8]{1,0:T(1,128)}, u32[]{:S(2)}) copy-start(s32[1,8]{1,0:T(1,128)} %refs_1_.5) | copy-start | bytes 100
  0.0 7.0 %copy-start.2 = (bf16[1,8,48,384]{3,2,1,0:T(8,128)(2,1)S(1)}, bf16[1,8,48,384]{3,2,1,0:T(8,128)(2,1)}, u32[]{:S(2)}) copy-start(bf16[1,8,48,384]{3,2,1,0:T(8,128)(2,1)} %param.5) | copy-start | bytes 884740
  1.2 18.7 %collective-permute-start.3 = (bf16[768,384]{1,0:T(8,128)(2,1)S(1)}, bf16[768,384]{1,0:T(8,128)(2,1)S(1)}, u32[]{:S(2)}, u32[]{:S(2)}) collective-permute-start(bf16[768,384]{1,0:T(8,128)(2,1)S(1)} %pad_maximum_fusion.refs_3_), channel_id=1, source_target_pairs={{0,4},{12,8},{1,5},{13,9},{2,6},{14,10},{3,7},{15,11},{16,20},{28,... | collective-permute-start | bytes 1769480 | tf_op jit(solution)/shard_map/ppermute | solution.py:21
  6.1 15.2 %collective-permute-start.1 = (bf16[768,384]{1,0:T(8,128)(2,1)S(1)}, bf16[768,384]{1,0:T(8,128)(2,1)S(1)}, u32[]{:S(2)}, u32[]{:S(2)}) collective-permute-start(bf16[768,384]{1,0:T(8,128)(2,1)S(1)} %pad_maximum_fusion.refs_3_), channel_id=1, source_target_pairs={{4,8},{8,4},{5,9},{9,5},{6,10},{10,6},{7,11},{11,7},{20,24},{24,20... | collective-permute-start | bytes 1769480 | tf_op jit(solution)/shard_map/ppermute | solution.py:21
  6.8 18.5 %collective-permute-start = (bf16[768,384]{1,0:T(8,128)(2,1)S(1)}, bf16[768,384]{1,0:T(8,128)(2,1)S(1)}, u32[]{:S(2)}, u32[]{:S(2)}) collective-permute-start(bf16[768,384]{1,0:T(8,128)(2,1)S(1)} %pad_maximum_fusion.refs_3_), channel_id=1, source_target_pairs={{0,2},{2,0},{1,3},{3,1},{4,6},{6,4},{5,7},{7,5},{8,10},{10,8},{9,1... | collective-permute-start | bytes 1769480 | tf_op jit(solution)/shard_map/ppermute | solution.py:25
  7.8 17.5 %collective-permute-start.6 = (bf16[400,384]{1,0:T(8,128)(2,1)}, bf16[400,384]{1,0:T(8,128)(2,1)S(1)}, u32[]{:S(2)}, u32[]{:S(2)}) collective-permute-start(bf16[400,384]{1,0:T(8,128)(2,1)} %pad_maximum_fusion.1), channel_id=1, source_target_pairs={{0,4},{12,8},{1,5},{13,9},{2,6},{14,10},{3,7},{15,11},{16,20},{28,... | collective-permute-start | bytes 921608 | tf_op jit(solution)/shard_map/ppermute | solution.py:21
  19.8 5.5 %collective-permute-start.4 = (bf16[768,384]{1,0:T(8,128)(2,1)S(1)}, bf16[768,384]{1,0:T(8,128)(2,1)S(1)}, u32[]{:S(2)}, u32[]{:S(2)}) collective-permute-start(bf16[768,384]{1,0:T(8,128)(2,1)S(1)} %collective-permute-done.3.refs_7_), channel_id=1, source_target_pairs={{0,2},{2,0},{1,3},{3,1},{4,6},{6,4},{5,7},{7,5},{8,10},{10,8},{9,1... | collective-permute-start | bytes 1769480 | tf_op jit(solution)/shard_map/ppermute | solution.py:25
  19.8 9.0 %collective-permute-start.5 = (bf16[768,384]{1,0:T(8,128)(2,1)S(1)}, bf16[768,384]{1,0:T(8,128)(2,1)}, u32[]{:S(2)}, u32[]{:S(2)}) collective-permute-start(bf16[768,384]{1,0:T(8,128)(2,1)S(1)} %collective-permute-done.3.refs_7_), channel_id=1, source_target_pairs={{4,8},{8,4},{5,9},{9,5},{6,10},{10,6},{7,11},{11,7},{20,24},{24,20... | collective-permute-start | bytes 1769480 | tf_op jit(solution)/shard_map/ppermute | solution.py:21
  21.3 4.1 %collective-permute-start.2 = (bf16[768,384]{1,0:T(8,128)(2,1)S(1)}, bf16[768,384]{1,0:T(8,128)(2,1)}, u32[]{:S(2)}, u32[]{:S(2)}) collective-permute-start(bf16[768,384]{1,0:T(8,128)(2,1)S(1)} %collective-permute-done.1.refs_5_), channel_id=1, source_target_pairs={{0,2},{2,0},{1,3},{3,1},{4,6},{6,4},{5,7},{7,5},{8,10},{10,8},{9,1... | collective-permute-start | bytes 1769480 | tf_op jit(solution)/shard_map/ppermute | solution.py:25
  25.4 0.7 %copy-start.7 = (s32[2]{0:T(128)S(1)}, s32[2]{0:T(128)}, u32[]{:S(2)}) copy-start(s32[2]{0:T(128)} %shard_map.55.refs_0_) | copy-start | bytes 28
  27.4 0.8 %copy-start = (f32[384,384]{1,0:T(8,128)}, f32[384,384]{1,0:T(8,128)S(1)}, u32[]{:S(2)}) copy-start(f32[384,384]{1,0:T(8,128)S(1)} %get-tuple-element.13.refs_5_) | copy-start | bytes 1769476
  28.2 0.7 %copy-start.3 = (f32[384,128]{1,0:T(8,128)}, f32[384,128]{1,0:T(8,128)S(1)}, u32[]{:S(2)}) copy-start(f32[384,128]{1,0:T(8,128)S(1)} %get-tuple-element.14.refs_6_) | copy-start | bytes 589828
  28.8 2.3 %collective-permute-start.7 = (bf16[768,384]{1,0:T(8,128)(2,1)}, bf16[768,384]{1,0:T(8,128)(2,1)}, u32[]{:S(2)}, u32[]{:S(2)}) collective-permute-start(bf16[768,384]{1,0:T(8,128)(2,1)} %collective-permute-done.5.refs_9_.refs_3_), channel_id=1, source_target_pairs={{0,2},{2,0},{1,3},{3,1},{4,6},{6,4},{5,7},{7,5},{8,10},{10,8},{9,1... | collective-permute-start | bytes 1769480 | tf_op jit(solution)/shard_map/ppermute | solution.py:25
  31.2 1.1 %copy-start.1 = (f32[384,384]{1,0:T(8,128)S(1)}, f32[384,384]{1,0:T(8,128)}, u32[]{:S(2)}) copy-start(f32[384,384]{1,0:T(8,128)} %copy-done) | copy-start | bytes 1769476
  32.3 0.9 %copy-start.4 = (f32[384,128]{1,0:T(8,128)S(1)}, f32[384,128]{1,0:T(8,128)}, u32[]{:S(2)}) copy-start(f32[384,128]{1,0:T(8,128)} %copy-done.3) | copy-start | bytes 589828
  33.2 0.7 %copy-start.6 = (s32[2]{0:T(128)S(1)}, s32[2]{0:T(128)}, u32[]{:S(2)}) copy-start(s32[2]{0:T(128)} %refs_0_.3) | copy-start | bytes 28
  35.6 21.5 %collective-permute-start.8 = (bf16[384,384]{1,0:T(8,128)(2,1)S(1)}, bf16[384,384]{1,0:T(8,128)(2,1)S(1)}, u32[]{:S(2)}, u32[]{:S(2)}) collective-permute-start(bf16[384,384]{1,0:T(8,128)(2,1)S(1)} %shard_map.58), channel_id=1, source_target_pairs={{4,0},{8,12},{5,1},{9,13},{6,2},{10,14},{7,3},{11,15},{20,16},{24,... | collective-permute-start | bytes 884744 | tf_op jit(solution)/shard_map/ppermute | solution.py:21
